TPU v7x, 32 devices: a whole 2x2x4 slice. The times are simulated.
32 devices in a mesh: dp: 8 (over y, x, core), tensor: 4 (over z).
Axes of the slice: x: 2, y: 2, z: 4, core: 2. Of those that a mesh axis runs over, the one named last changes fastest.
Arguments:
- block_input: bfloat16 [2048, 2048], P('dp'), may hold values from -6 to 6
- segment_ids: int32 [8, 256], P('dp'), may hold values from 0 to 2, never falling along the last dimension, each value on 1 to 192 neighbouring positions
- expert_ids: int32 [2048, 8], P('dp'), may hold values from 0 to 31, all different within a row; in each aligned block of 256 rows (0 to 255, 256 to 511, ...) at most 128 rows name the same one
- attn_gain: float32 [2048], replicated, may hold values from 0.25 to 1.75
- query_weight: bfloat16 [2048, 4096], P(None, 'tensor'), may hold values from -0.125 to 0.125
- key_projection: bfloat16 [2048, 512], P(None, 'tensor'), may hold values from -0.125 to 0.125
- value_projection: bfloat16 [2048, 512], P(None, 'tensor'), may hold values from -0.125 to 0.125
- query_norm_gain: float32 [128], replicated, may hold values from 0.25 to 1.75
- key_norm_gain: float32 [128], replicated, may hold values from 0.25 to 1.75
- output_projection: bfloat16 [2048, 4096], P(None, 'tensor'), may hold values from -0.375 to 0.375
- ffn_gain: float32 [2048], replicated, may hold values from 0.25 to 1.75
- router_weight: bfloat16 [2048, 32], replicated, may hold values from -0.0625 to 0.0625
- gate_experts: bfloat16 [32, 2048, 768], P('dp', None, 'tensor'), may hold values from -0.125 to 0.125
- up_experts: bfloat16 [32, 2048, 768], P('dp', None, 'tensor'), may hold values from -0.125 to 0.125
- down_experts: bfloat16 [32, 768, 2048], P('dp', 'tensor'), may hold values from -0.4375 to 0.4375
- out_grad: bfloat16 [2048, 2048], P('dp'), may hold values from -6 to 6
Outputs:
- block_output: bfloat16 [2048, 2048], P('dp')
- input_grad: bfloat16 [2048, 2048], P('dp')
- attn_gain_grad: float32 [2048], P('dp')
- query_weight_grad: float32 [2048, 4096], P('dp', 'tensor')
- key_weight_grad: float32 [2048, 512], P('dp', 'tensor')
- value_weight_grad: float32 [2048, 512], P('dp', 'tensor')
- query_gain_grad: float32 [128], P('dp')
- key_gain_grad: float32 [128], P('dp')
- out_weight_grad: float32 [2048, 4096], P('dp', 'tensor')
- ffn_gain_grad: float32 [2048], P('dp')
- router_weight_grad: float32 [2048, 32], P('dp')
- gate_experts_grad: float32 [32, 2048, 768], P('dp', None, 'tensor')
- up_experts_grad: float32 [32, 2048, 768], P('dp', None, 'tensor')
- down_experts_grad: float32 [32, 768, 2048], P('dp', 'tensor')
Inputs may be any that keep to these rules, and one draw needn't show every extreme that they name: `segment_ids`: segment ids never fall along a row; each segment holds 1 to 192 tokens and one of each row holds exactly 192. `expert_ids`: each row names 8 different experts. No expert is named by more than 128 of the rows of one index of dp, a bound that some block reaches by the rows of some index of dp.
All inputs are finite; a program needn't handle non-finite values.
Results may differ from a plain program's by a relative error of at most 0.03.
Values may be sent and summed in bfloat16 or wider, within the bound.
No kernel may reach another device: no remote copies, remote signals or barrier semaphores. Data moves between devices by JAX's collectives and lax.ppermute only.
A program may use at most 320 MiB of HBM per device.

v0:
```python
import jax
import jax.numpy as jnp
from jax import lax
from jax.sharding import PartitionSpec as P

EPS = 1e-06
THETA = 1000000.0
F32 = jnp.float32
BF16 = jnp.bfloat16


def rms_scale(values):
    return lax.rsqrt(jnp.mean(values * values, axis=-1, keepdims=True) + EPS)


def norm_reverse(grad_rows, normed, scale_rows):
    return scale_rows * (grad_rows - normed * jnp.mean(grad_rows * normed, axis=-1, keepdims=True))


def dot_nn(a, b):
    return lax.dot_general(a, b, (((1,), (0,)), ((), ())), preferred_element_type=F32)


def dot_nt(a, b):
    return lax.dot_general(a, b, (((1,), (1,)), ((), ())), preferred_element_type=F32)


def dot_tn(a, b):
    return lax.dot_general(a, b, (((0,), (0,)), ((), ())), preferred_element_type=F32)


def swap(value, bit, count):
    return lax.ppermute(value, "dp", [(i, i ^ bit) for i in range(count)])


def shift(value, step, count):
    return lax.ppermute(value, "tensor", [(i, (i + step) % count) for i in range(count)])


def gather_dp(shard, count):
    if count == 8:
        half = shard.shape[0] // 2
        along_x = swap(shard, 2, count)
        along_y = swap(shard, 4, count)
        mate = swap(shard, 1, count)
        diag_lo = swap(along_y[:half], 2, count)
        diag_hi = swap(along_x[half:], 4, count)
        mate_x = swap(along_x, 1, count)
        mate_y = swap(along_y, 1, count)
        diag = jnp.concatenate([diag_lo, diag_hi], 0)
        mate_d = swap(diag, 1, count)
        return [shard, mate, along_x, mate_x, along_y, mate_y, diag, mate_d]
    return [lax.all_gather(shard, "dp", axis=0, tiled=True)]


def add_b(a, b):
    return (a.astype(F32) + b.astype(F32)).astype(BF16)


def scatter_dp(rows, count):
    if count == 8:
        size = rows.shape[0] // count
        half = size // 2
        chunks = [rows[r * size : (r + 1) * size] for r in range(count)]
        pair = {}
        for r in (6, 4, 2, 0):
            pair[r] = add_b(chunks[r], swap(chunks[r + 1], 1, count))
        from_x = swap(pair[6][:half], 2, count)
        from_y = swap(pair[6][half:], 4, count)
        to_y = jnp.concatenate([add_b(pair[4][:half], from_x), pair[4][half:]], 0)
        to_x = jnp.concatenate([pair[2][:half], add_b(pair[2][half:], from_y)], 0)
        got_x = swap(to_x, 2, count)
        got_y = swap(to_y, 4, count)
        return (pair[0].astype(F32) + got_x.astype(F32) + got_y.astype(F32)).astype(BF16)
    return lax.psum_scatter(rows, "dp", scatter_dimension=0, tiled=True)


def gather_z(shard, count):
    if count == 4:
        half = shard.shape[1] // 2
        prev = shift(shard, 1, count)
        after = shift(shard, -1, count)
        far_lo = shift(prev[:, :half], 1, count)
        far_hi = shift(after[:, half:], -1, count)
        far = jnp.concatenate([far_lo, far_hi], 1)
        return jnp.concatenate([shard, after, far, prev], 0)
    return jnp.concatenate([shard] + [shift(shard, -r, count) for r in range(1, count)], 0)


def scatter_z(rows, count):
    size = rows.shape[0] // count
    block = [rows[r * size : (r + 1) * size] for r in range(count)]
    if count == 4:
        half = rows.shape[1] // 2
        lo = shift(block[2][:, :half], 1, count)
        hi = shift(block[2][:, half:], -1, count)
        up = jnp.concatenate([add_b(block[1][:, :half], lo), block[1][:, half:]], 1)
        down = jnp.concatenate([block[3][:, :half], add_b(block[3][:, half:], hi)], 1)
        got_up = shift(up, 1, count)
        got_down = shift(down, -1, count)
        return block[0].astype(F32) + got_up.astype(F32) + got_down.astype(F32)
    total = block[0].astype(F32)
    for r in range(1, count):
        total = total + shift(block[r], r, count).astype(F32)
    return total


def roll_rows(rows, amount):
    return jnp.roll(rows, amount, axis=0)


def rope_apply(values, cos_rows, sin_rows):
    half = values.shape[-1] // 2
    low, high = (values[..., :half], values[..., half:])
    c, s = (cos_rows[:, None, :], sin_rows[:, None, :])
    return jnp.concatenate([low * c - high * s, high * c + low * s], axis=-1)


def rope_back(values, cos_rows, sin_rows):
    half = values.shape[-1] // 2
    low, high = (values[..., :half], values[..., half:])
    c, s = (cos_rows[:, None, :], sin_rows[:, None, :])
    return jnp.concatenate([low * c + high * s, high * c - low * s], axis=-1)


def local(
    block_input,
    segment_ids,
    expert_ids,
    attn_gain,
    query_weight,
    key_projection,
    value_projection,
    query_norm_gain,
    key_norm_gain,
    output_projection,
    ffn_gain,
    router_weight,
    gate_experts,
    up_experts,
    down_experts,
    out_grad,
):
    tokens, width = block_input.shape
    head_dim = query_norm_gain.shape[0]
    experts_dev, _, hidden_dev = gate_experts.shape
    n_dp = lax.axis_size("dp")
    n_t = lax.axis_size("tensor")
    num_experts = experts_dev * n_dp
    part = tokens // n_t
    flat = experts_dev * hidden_dev
    t_index = lax.axis_index("tensor")
    d_index = lax.axis_index("dp")
    turn = t_index * part
    scale_value = head_dim ** (-0.5)
    x_rows = roll_rows(block_input, -turn)
    seg = roll_rows(segment_ids[0], -turn)
    ids = roll_rows(expert_ids, -turn)
    dy_rows = roll_rows(out_grad, -turn)
    order = (jnp.arange(tokens, dtype=jnp.int32) + turn) % tokens
    dy_chunks = gather_dp(dy_rows, n_dp)
    ids_all = jnp.concatenate(gather_dp(ids, n_dp), 0)
    dy_all = jnp.concatenate(dy_chunks, 0)
    inputs_f = x_rows.astype(F32)
    scale_one = rms_scale(inputs_f)
    normed_one = inputs_f * scale_one
    attn_in = (normed_one * attn_gain).astype(BF16)
    same = seg[:, None] == seg[None, :]
    earlier = order[None, :] < order[:, None]
    positions = jnp.sum((same & earlier).astype(jnp.int32), axis=1)
    half_dim = head_dim // 2
    frequency = THETA ** (-(jnp.arange(half_dim, dtype=F32) * 2.0) / head_dim)
    angles = positions.astype(F32)[:, None] * frequency[None, :]
    cos_rows, sin_rows = (jnp.cos(angles), jnp.sin(angles))
    allowed = same & (order[None, :] <= order[:, None])
    q_raw = dot_nn(attn_in, query_weight).reshape(tokens, -1, head_dim)
    q_scale = rms_scale(q_raw)
    q_hat = q_raw * q_scale
    k_raw = dot_nn(attn_in, key_projection).reshape(tokens, -1, head_dim)
    k_scale = rms_scale(k_raw)
    k_hat = k_raw * k_scale
    k_rot = rope_apply(k_hat * key_norm_gain, cos_rows, sin_rows).astype(BF16)
    v_rows = dot_nn(attn_in, value_projection).astype(BF16).reshape(tokens, -1, head_dim)
    heads = q_raw.shape[1]
    kv = k_raw.shape[1]
    group = heads // kv
    q_rot = rope_apply(q_hat * query_norm_gain, cos_rows, sin_rows).astype(BF16)
    q_rot = q_rot.reshape(tokens, kv, group, head_dim)
    scores = jnp.einsum("qkgd,skd->kgqs", q_rot, k_rot, preferred_element_type=F32) * scale_value
    scores = jnp.where(allowed, scores, -jnp.inf)
    top = jnp.max(scores, axis=-1, keepdims=True)
    weights = jnp.exp(scores - top)
    totals = jnp.sum(weights, axis=-1, keepdims=True)
    probs = weights / totals
    probs_b = probs.astype(BF16)
    attn_out = jnp.einsum("kgqs,skd->qkgd", probs_b, v_rows, preferred_element_type=F32)
    attn_out = attn_out.astype(BF16)
    attn_flat = attn_out.reshape(tokens, heads * head_dim)
    attn_part = dot_nt(attn_flat, output_projection).astype(BF16)
    attn_sum = scatter_z(attn_part, n_t)
    x_own = inputs_f[:part]
    ids_own = ids[:part]
    middle = x_own + attn_sum
    scale_two = rms_scale(middle)
    normed_two = middle * scale_two
    ffn_own = (normed_two * ffn_gain).astype(BF16)
    ffn_rows = gather_z(ffn_own, n_t)
    x_all = jnp.concatenate(gather_dp(ffn_rows, n_dp), 0)

    def router(rows, chosen):
        logits = dot_nn(rows, router_weight)
        raised = jnp.exp(logits - jnp.max(logits, axis=-1, keepdims=True))
        prob = raised / jnp.sum(raised, axis=-1, keepdims=True)
        names = jnp.arange(num_experts, dtype=jnp.int32)
        mask = jnp.any(chosen[:, :, None] == names[None, None, :], axis=1).astype(F32)
        total = jnp.sum(prob * mask, axis=-1, keepdims=True)
        return (prob, mask, total, prob * mask / total)

    prob_own, mask_own, total_own, gate_own = router(ffn_own, ids_own)
    gate_all = router(x_all, ids_all)[3]
    owner = d_index * experts_dev + jnp.arange(flat, dtype=jnp.int32) // hidden_dev
    names = jnp.arange(num_experts, dtype=jnp.int32)
    place = (names[:, None] == owner[None, :]).astype(F32)
    gate_wide = jnp.dot(gate_all, place, precision=lax.Precision.HIGHEST)
    wg = jnp.transpose(gate_experts, (0, 2, 1)).reshape(flat, width)
    wu = jnp.transpose(up_experts, (0, 2, 1)).reshape(flat, width)
    wd = down_experts.reshape(flat, width)
    d_hidden = dot_nt(dy_all, wd)
    gate_pre = dot_nt(x_all, wg)
    up_pre = dot_nt(x_all, wu)
    sig = jax.nn.sigmoid(gate_pre)
    act = gate_pre * sig
    hidden = act * up_pre
    hidden_g = (hidden * gate_wide).astype(BF16)
    gate_grads = lax.dot_general(
        hidden * d_hidden, place, (((1,), (1,)), ((), ())), precision=lax.Precision.HIGHEST
    )
    hidden_grad = d_hidden * gate_wide
    dg = (hidden_grad * up_pre * sig * (1.0 + gate_pre * (1.0 - sig))).astype(BF16)
    du = (hidden_grad * act).astype(BF16)
    back = (dot_nn(dg, wg) + dot_nn(du, wu)).astype(BF16)
    pad = -num_experts % 128
    back = jnp.concatenate([back, jnp.pad(gate_grads, ((0, 0), (0, pad))).astype(BF16)], 1)
    back_sum = scatter_dp(back, n_dp)
    back_own = scatter_z(back_sum, n_t)
    ffn_back = back_own[:, :width]
    gate_grad = back_own[:, width : width + num_experts]
    mix = dot_nn(hidden_g, wd).astype(BF16)
    mix_sum = scatter_dp(mix, n_dp)
    mix_own = scatter_z(mix_sum, n_t)
    block_out = gather_z((middle + mix_own).astype(BF16), n_t)
    block_output = roll_rows(block_out, turn)
    down_grad = dot_tn(hidden_g, dy_all).reshape(experts_dev, hidden_dev, width)
    gate_w_grad = dot_tn(dg, x_all).reshape(experts_dev, hidden_dev, width).transpose(0, 2, 1)
    up_w_grad = dot_tn(du, x_all).reshape(experts_dev, hidden_dev, width).transpose(0, 2, 1)
    select_grad = (gate_grad - jnp.sum(gate_grad * gate_own, axis=-1, keepdims=True)) / total_own
    prob_grad = mask_own * select_grad
    logit_grad = (
        prob_own * (prob_grad - jnp.sum(prob_grad * prob_own, axis=-1, keepdims=True))
    ).astype(BF16)
    router_part = dot_tn(ffn_own, logit_grad)
    ffn_grad = ffn_back + dot_nt(logit_grad, router_weight)
    ffn_gain_part = jnp.sum(ffn_grad * normed_two, axis=0)
    mid_grad = dy_rows[:part].astype(F32) + norm_reverse(ffn_grad * ffn_gain, normed_two, scale_two)
    mid_rows = gather_z(mid_grad.astype(BF16), n_t)
    d_attn = dot_nn(mid_rows, output_projection).astype(BF16)
    d_out = d_attn.reshape(tokens, kv, group, head_dim)
    delta = jnp.sum(d_out.astype(F32) * attn_out.astype(F32), axis=-1)
    delta = jnp.transpose(delta, (1, 2, 0))[..., None]
    v_grad = jnp.einsum("kgqs,qkgd->skd", probs_b, d_out, preferred_element_type=F32)
    p_grad = jnp.einsum("qkgd,skd->kgqs", d_out, v_rows, preferred_element_type=F32)
    s_grad = (probs * (p_grad - delta) * scale_value).astype(BF16)
    q_grad = jnp.einsum("kgqs,skd->qkgd", s_grad, k_rot, preferred_element_type=F32)
    k_grad = jnp.einsum("kgqs,qkgd->skd", s_grad, q_rot, preferred_element_type=F32)
    q_back = rope_back(q_grad.reshape(tokens, heads, head_dim), cos_rows, sin_rows)
    q_gain_part = jnp.sum(q_back * q_hat, axis=(0, 1))
    q_raw_grad = norm_reverse(q_back * query_norm_gain, q_hat, q_scale).astype(BF16)
    q_raw_grad = q_raw_grad.reshape(tokens, -1)
    k_back = rope_back(k_grad, cos_rows, sin_rows)
    k_gain_part = jnp.sum(k_back * k_hat, axis=(0, 1))
    k_raw_grad = norm_reverse(k_back * key_norm_gain, k_hat, k_scale).astype(BF16)
    k_raw_grad = k_raw_grad.reshape(tokens, -1)
    v_grad_b = v_grad.astype(BF16).reshape(tokens, -1)
    in_part = (
        dot_nt(q_raw_grad, query_weight)
        + dot_nt(k_raw_grad, key_projection)
        + dot_nt(v_grad_b, value_projection)
    ).astype(BF16)
    attn_in_grad = scatter_z(in_part, n_t)
    normed_own = normed_one[:part]
    attn_gain_part = jnp.sum(attn_in_grad * normed_own, axis=0)
    input_own = mid_grad + norm_reverse(attn_in_grad * attn_gain, normed_own, scale_one[:part])
    input_grad = roll_rows(gather_z(input_own.astype(BF16), n_t), turn)

    def weight_grad(rows_dp, columns_dp):
        return dot_tn(jnp.concatenate(rows_dp, 0), jnp.concatenate(columns_dp, 0))

    slab = width // n_dp

    def spread(rows):
        if n_dp != 8:
            return [lax.all_to_all(rows, "dp", split_axis=1, concat_axis=0, tiled=True)]
        out = []
        for r in range(n_dp):
            piece = lax.dynamic_slice_in_dim(rows, (d_index ^ r) * slab, slab, 1)
            out.append(piece if r == 0 else swap(piece, r, n_dp))
        return out

    attn_in_slab = spread(attn_in)
    mid_slab = spread(mid_rows)
    out_weight_grad = weight_grad(mid_slab, gather_dp(attn_flat, n_dp))
    qkv_grad = jnp.concatenate([q_raw_grad, k_raw_grad, v_grad_b], 1)
    qkv_w = weight_grad(attn_in_slab, gather_dp(qkv_grad, n_dp))
    q_cols = heads * head_dim
    kv_cols = kv * head_dim
    query_weight_grad = qkv_w[:, :q_cols]
    key_weight_grad = qkv_w[:, q_cols : q_cols + kv_cols]
    value_weight_grad = qkv_w[:, q_cols + kv_cols :]
    router_sum = lax.psum(
        lax.psum_scatter(router_part.astype(BF16), "dp", scatter_dimension=0, tiled=True), "tensor"
    ).astype(F32)
    gains = jnp.concatenate([attn_gain_part, ffn_gain_part, q_gain_part, k_gain_part])
    gains = lax.psum(gains, ("dp", "tensor"))

    def mine(vector):
        size = vector.shape[0] // n_dp
        return lax.dynamic_slice_in_dim(vector, d_index * size, size, 0)

    return (
        block_output,
        input_grad,
        mine(gains[:width]),
        query_weight_grad,
        key_weight_grad,
        value_weight_grad,
        mine(gains[2 * width : 2 * width + head_dim]),
        mine(gains[2 * width + head_dim :]),
        out_weight_grad,
        mine(gains[width : 2 * width]),
        router_sum,
        gate_w_grad,
        up_w_grad,
        down_grad,
    )


def solution(mesh):
    return jax.shard_map(
        local,
        mesh=mesh,
        in_specs=(
            P("dp", None),
            P("dp", None),
            P("dp", None),
            P(),
            P(None, "tensor"),
            P(None, "tensor"),
            P(None, "tensor"),
            P(),
            P(),
            P(None, "tensor"),
            P(),
            P(),
            P("dp", None, "tensor"),
            P("dp", None, "tensor"),
            P("dp", "tensor", None),
            P("dp", None),
        ),
        out_specs=(
            P("dp", None),
            P("dp", None),
            P("dp"),
            P("dp", "tensor"),
            P("dp", "tensor"),
            P("dp", "tensor"),
            P("dp"),
            P("dp"),
            P("dp", "tensor"),
            P("dp"),
            P("dp", None),
            P("dp", None, "tensor"),
            P("dp", None, "tensor"),
            P("dp", "tensor", None),
        ),
        check_vma=False,
    )
```

profile of v0, /device:TPU:0, one launch (start us, length us, event | category | flops | bytes accessed | tf_op | source)
XLA Modules:
  0.0 638.1 jit_solution(17216061805389194970)
XLA Ops:
  75.1 4.1 collective-permute-done.76
  83.7 6.4 %collective-permute-done.1 = bf16[64,2048]{1,0:T(8,128)(2,1)S(1)} collective-permute-done((bf16[64,2048]{1,0:T(8,128)(2,1)S(1)}, bf16[64,2048]{1,0:T(8,128)(2,1)S(1)}, u32[]{:S(2)}, u32[]{:S(2)}) %collective-permute-start.1) | collective-permute-done | bytes 262176 | tf_op jit(solution)/shard_map/ppermute | solution.py:37
  121.8 9.1 %collective-permute-done.43 = bf16[256,2048]{1,0:T(8,128)(2,1)S(1)} collective-permute-done((bf16[256,2048]{1,0:T(8,128)(2,1)S(1)}, bf16[256,2048]{1,0:T(8,128)(2,1)S(1)}, u32[]{:S(2)}, u32[]{:S(2)}) %collective-permute-start.43) | collective-permute-done | bytes 1048608 | tf_op jit(solution)/shard_map/ppermute | solution.py:33
  144.5 25.2 %collective-permute-done.45 = bf16[128,2048]{1,0:T(8,128)(2,1)S(1)} collective-permute-done((bf16[128,2048]{1,0:T(8,128)(2,1)S(1)}, bf16[128,2048]{1,0:T(8,128)(2,1)S(1)}, u32[]{:S(2)}, u32[]{:S(2)}) %collective-permute-start.45) | collective-permute-done | bytes 524320 | tf_op jit(solution)/shard_map/ppermute | solution.py:33
  181.9 5.3 collective-permute-done.13
  189.9 9.1 %fusion.111 = f32[2048,768]{1,0:T(8,128)S(1)} fusion(bf16[2048,2048]{1,0:T(8,128)(2,1)} %constant_dynamic-update-slice_fusion.21, bf16[768,2048]{1,0:T(8,128)(2,1)S(1)} %bitcast.211), kind=kOutput, calls=%fused_computation.348 | convolution fusion | flops 6442450944 | bytes 17825792 | tf_op jit(solution)/shard_map/dot_general | solution.py:25
  204.4 8.6 %fusion.110 = f32[2048,768]{1,0:T(8,128)} fusion(bf16[2048,2048]{1,0:T(8,128)(2,1)S(1)} %constant_dynamic-update-slice_fusion, bf16[768,2048]{1,0:T(8,128)(2,1)S(1)} %bitcast.209), kind=kOutput, calls=%fused_computation.347 | convolution fusion | flops 6442450944 | bytes 17825792 | tf_op jit(solution)/shard_map/dot_general | solution.py:25
  213.0 8.6 %fusion.109 = f32[2048,768]{1,0:T(8,128)} fusion(bf16[2048,2048]{1,0:T(8,128)(2,1)S(1)} %constant_dynamic-update-slice_fusion, bf16[768,2048]{1,0:T(8,128)(2,1)S(1)} %bitcast.192), kind=kOutput, calls=%fused_computation.346 | convolution fusion | flops 6442450944 | bytes 17825792 | tf_op jit(solution)/shard_map/dot_general | solution.py:25
  221.6 7.6 %fusion.7 = bf16[2048,32]{0,1:T(8,128)(2,1)} fusion(f32[2048,768]{1,0:T(8,128)S(1)} %fusion.111, f32[2048,768]{1,0:T(8,128)S(1)} %copy-done.106, s32[768]{0:T(1024)S(1)} %fusion.79, f32[2048,768]{1,0:T(8,128)} %fusion.109), kind=kOutput, calls=%fused_computation.17 | convolution fusion | flops 613507072 | bytes 19008512 | tf_op jit(solution)/shard_map/dot_general | solution.py:235
  231.2 10.7 %multiply_convert_fusion = (bf16[2048,768]{1,0:T(8,128)(2,1)S(1)}, bf16[2048,768]{1,0:T(8,128)(2,1)S(1)}, bf16[2048,768]{1,0:T(8,128)(2,1)}) fusion(f32[2048,768]{1,0:T(8,128)} %copy-done.105, f32[2048,768]{1,0:T(8,128)} %fusion.109, f32[2048,768]{1,0:T(8,128)} %fusion.110, s32[768]{0:T(1024)S(1)} %fusion.79, f32[2048]{0:T(1024)S(1)} %fusion.76, ...), kind=kOutput, calls=%fused_computation.7 | convolution fusion | flops 631005184 | bytes 28666880 | tf_op jit(solution)/shard_map/dot_general | solution.py:224
  242.0 9.5 %fusion.112 = f32[2048,2048]{1,0:T(8,128)} fusion(bf16[2048,768]{1,0:T(8,128)(2,1)S(1)} %get-tuple-element.34, bf16[768,2048]{1,0:T(8,128)(2,1)S(1)} %bitcast.193), kind=kOutput, calls=%fused_computation.349 | convolution fusion | flops 6442450944 | bytes 23068672 | tf_op jit(solution)/shard_map/dot_general | solution.py:21
  251.5 12.6 %add_convert_fusion = bf16[2048,2048]{1,0:T(8,128)(2,1)} fusion(f32[2048,2048]{1,0:T(8,128)} %fusion.112, bf16[2048,768]{1,0:T(8,128)(2,1)S(1)} %get-tuple-element.33, bf16[768,2048]{1,0:T(8,128)(2,1)S(1)} %bitcast.210), kind=kOutput, calls=%fused_computation.2 | convolution fusion | flops 6450839552 | bytes 31457280 | tf_op jit(solution)/shard_map/dot_general | solution.py:21
  264.0 8.0 %fusion.1 = bf16[2048,2176]{1,0:T(8,128)(2,1)} fusion(bf16[2048,32]{1,0:T(8,128)(2,1)S(1)} %copy-done.26, bf16[2048,2048]{1,0:T(8,128)(2,1)} %add_convert_fusion), kind=kLoop, calls=%fused_computation.3 | loop fusion | flops 26738688 | bytes 17432576 | tf_op jit(solution)/shard_map/concatenate | solution.py:243
  272.0 4.2 fusion.94
  276.7 9.2 %convolution_convert_fusion = bf16[2048,2048]{1,0:T(8,128)(2,1)S(1)} fusion(bf16[2048,768]{1,0:T(8,128)(2,1)} %get-tuple-element.35, bf16[768,2048]{1,0:T(8,128)(2,1)S(1)} %bitcast.212), kind=kOutput, calls=%fused_computation.4 | convolution fusion | flops 6446645248 | bytes 14680064 | tf_op jit(solution)/shard_map/dot_general | solution.py:21
  288.4 10.5 %fusion.116 = f32[768,2048]{1,0:T(8,128)} fusion(bf16[2048,768]{1,0:T(8,128)(2,1)} %copy-done.109, bf16[2048,2048]{1,0:T(8,128)(2,1)S(1)} %bitcast.200), kind=kOutput, calls=%fused_computation.353 | convolution fusion | flops 6442450944 | bytes 17825792 | tf_op jit(solution)/shard_map/dot_general | solution.py:29
  310.9 8.4 %collective-permute-done.30 = bf16[128,2048]{1,0:T(8,128)(2,1)} collective-permute-done((bf16[128,2048]{1,0:T(8,128)(2,1)}, bf16[128,2048]{1,0:T(8,128)(2,1)}, u32[]{:S(2)}, u32[]{:S(2)}) %collective-permute-start.30) | collective-permute-done | bytes 524320 | tf_op jit(solution)/shard_map/ppermute | solution.py:33
  323.0 7.7 %collective-permute-done.54 = bf16[128,2176]{1,0:T(8,128)(2,1)S(1)} collective-permute-done((bf16[128,2176]{1,0:T(8,128)(2,1)S(1)}, bf16[128,2176]{1,0:T(8,128)(2,1)S(1)}, u32[]{:S(2)}, u32[]{:S(2)}) %collective-permute-start.54) | collective-permute-done | bytes 557088 | tf_op jit(solution)/shard_map/ppermute | solution.py:33
  337.4 10.7 %fusion.117 = f32[768,2048]{1,0:T(8,128)} fusion(bf16[2048,768]{1,0:T(8,128)(2,1)} %copy-done.108, bf16[2048,2048]{1,0:T(8,128)(2,1)S(1)} %bitcast.200), kind=kOutput, calls=%fused_computation.354 | convolution fusion | flops 6442450944 | bytes 17825792 | tf_op jit(solution)/shard_map/dot_general | solution.py:29
  348.1 9.2 %collective-permute-done.31 = bf16[256,2048]{1,0:T(8,128)(2,1)S(1)} collective-permute-done((bf16[256,2048]{1,0:T(8,128)(2,1)S(1)}, bf16[256,2048]{1,0:T(8,128)(2,1)S(1)}, u32[]{:S(2)}, u32[]{:S(2)}) %collective-permute-start.31) | collective-permute-done | bytes 1048608 | tf_op jit(solution)/shard_map/ppermute | solution.py:33
  359.3 20.0 %collective-permute-done.55 = bf16[256,2176]{1,0:T(8,128)(2,1)S(1)} collective-permute-done((bf16[256,2176]{1,0:T(8,128)(2,1)S(1)}, bf16[256,2176]{1,0:T(8,128)(2,1)S(1)}, u32[]{:S(2)}, u32[]{:S(2)}) %collective-permute-start.55) | collective-permute-done | bytes 1114144 | tf_op jit(solution)/shard_map/ppermute | solution.py:33
  395.1 11.0 %fusion.118 = f32[768,2048]{1,0:T(8,128)} fusion(bf16[2048,768]{1,0:T(8,128)(2,1)S(1)} %copy-done.107, bf16[2048,2048]{1,0:T(8,128)(2,1)} %constant_dynamic-update-slice_fusion.21), kind=kOutput, calls=%fused_computation.355 | convolution fusion | flops 6442450944 | bytes 17825792 | tf_op jit(solution)/shard_map/dot_general | solution.py:29
  416.8 7.9 %collective-permute-done.60 = bf16[64,2048]{1,0:T(8,128)(2,1)S(1)} collective-permute-done((bf16[64,2048]{1,0:T(8,128)(2,1)S(1)}, bf16[64,2048]{1,0:T(8,128)(2,1)S(1)}, u32[]{:S(2)}, u32[]{:S(2)}) %collective-permute-start.60) | collective-permute-done | bytes 262176 | tf_op jit(solution)/shard_map/ppermute | solution.py:37
  428.1 4.8 collective-permute-start.62
  433.6 15.8 %reduce-scatter.2.cloned.1.call-done = bf16[256,32]{0,1:T(8,128)(2,1)} async-done(((bf16[2048,32]{0,1:T(8,128)(2,1)}), bf16[256,32]{0,1:T(8,128)(2,1)}) %reduce-scatter.2.cloned.1.call-update) | async-done | bytes 16400 | tf_op jit(solution)/shard_map/reduce_scatter | solution.py:320
  449.4 19.5 %psum.15 = bf16[256,32]{0,1:T(8,128)(2,1)S(1)} all-reduce(bf16[256,32]{0,1:T(8,128)(2,1)} %reduce-scatter.2.cloned.1.call-done), channel_id=1, replica_groups=mesh['dp'=8,'tensor'=4] {'tensor'}, use_global_device_ids=true, to_apply=%region_29.31 | all-reduce | flops 8192 | bytes 32768 | tf_op jit(solution)/shard_map/psum | solution.py:319
  509.5 5.9 collective-permute-start.67
  516.8 5.0 collective-permute-done.67
  539.3 39.3 %psum.14 = f32[4352]{0:T(1024)S(1)} all-reduce(f32[4352]{0:T(1024)S(1)} %pad_maximum_fusion.24), channel_id=1, replica_groups=mesh['dp'=8,'tensor'=4] {'dp','tensor'}, use_global_device_ids=true, to_apply=%region_27.29 | all-reduce | flops 4352 | bytes 34816 | tf_op jit(solution)/shard_map/psum | solution.py:323
  583.2 10.7 %collective-permute-done.69 = bf16[64,2048]{1,0:T(8,128)(2,1)S(1)} collective-permute-done((bf16[64,2048]{1,0:T(8,128)(2,1)S(1)}, bf16[64,2048]{1,0:T(8,128)(2,1)S(1)}, u32[]{:S(2)}, u32[]{:S(2)}) %collective-permute-start.69) | collective-permute-done | bytes 262176 | tf_op jit(solution)/shard_map/ppermute | solution.py:37
  610.8 7.6 %fusion.33 = bf16[256,2048]{1,0:T(8,128)(2,1)} fusion(s32[]{:T(128)S(6)} %select_n.114, bf16[64,2048]{1,0:T(8,128)(2,1)} %get-tuple-element.107, bf16[64,2048]{1,0:T(8,128)(2,1)S(1)} %collective-permute-done.36, bf16[64,1024]{1,0:T(8,128)(2,1)S(1)} %collective-permute-done.38, bf16[64,1024]{1,0:T(8,128)(2,1)S(1)} %collective-permute-done.39, ...), kind=kLoop, calls=%fused_computation.92 | loop fusion | flops 10485760 | bytes 2097156 | tf_op jit(solution)/shard_map/jit(_roll_dynamic)/concatenate | solution.py:109
  618.6 6.5 %fusion.23 = bf16[256,2048]{1,0:T(8,128)(2,1)} fusion(s32[]{:T(128)S(6)} %select_n.114, bf16[64,2048]{1,0:T(8,128)(2,1)S(1)} %get-tuple-element.106, bf16[64,2048]{1,0:T(8,128)(2,1)S(1)} %collective-permute-done.68, bf16[64,1024]{1,0:T(8,128)(2,1)S(1)} %collective-permute-done.70, bf16[64,1024]{1,0:T(8,128)(2,1)S(1)} %collective-permute-done.71, ...), kind=kLoop, calls=%fused_computation.82 | loop fusion | flops 10485760 | bytes 2097156 | tf_op jit(solution)/shard_map/jit(_roll_dynamic)/concatenate | solution.py:109
  (648 shorter events, 282.4 us)
Async XLA Ops:
  7.2 442.2 %reduce-scatter.2.cloned.1.call-start = ((), (), s32[]{:S(2)}) async-start(), calls=%async_computation.1 | async-start | bytes 147456 | tf_op jit(solution)/shard_map/reduce_scatter | solution.py:320
  8.8 44.6 %collective-permute-start.16 = (s32[256,8]{0,1:T(8,128)S(1)}, s32[256,8]{0,1:T(8,128)S(1)}, u32[]{:S(2)}, u32[]{:S(2)}) collective-permute-start(s32[256,8]{0,1:T(8,128)S(1)} %get-tuple-element.28), channel_id=1, source_target_pairs={{0,4},{4,0},{8,12},{12,8},{16,20},{20,16},{24,28},{28,24},{1,5},{5... | collective-permute-start | bytes 24584 | tf_op jit(solution)/shard_map/ppermute | solution.py:33
  9.3 43.6 %collective-permute-start.17 = (s32[256,8]{0,1:T(8,128)S(1)}, s32[256,8]{0,1:T(8,128)S(1)}, u32[]{:S(2)}, u32[]{:S(2)}) collective-permute-start(s32[256,8]{0,1:T(8,128)S(1)} %get-tuple-element.28), channel_id=1, source_target_pairs={{0,8},{4,12},{8,0},{12,4},{16,24},{20,28},{24,16},{28,20},{1,9},{5... | collective-permute-start | bytes 24584 | tf_op jit(solution)/shard_map/ppermute | solution.py:33
  11.8 38.7 %collective-permute-start.19 = (s32[256,8]{0,1:T(8,128)S(1)}, s32[256,8]{0,1:T(8,128)S(1)}, u32[]{:S(2)}, u32[]{:S(2)}) collective-permute-start(s32[256,8]{0,1:T(8,128)S(1)} %get-tuple-element.28), channel_id=1, source_target_pairs={{0,16},{4,20},{8,24},{12,28},{16,0},{20,4},{24,8},{28,12},{1,17},{... | collective-permute-start | bytes 24584 | tf_op jit(solution)/shard_map/ppermute | solution.py:33
  31.7 68.2 %collective-permute-start.94 = (bf16[256,1024]{0,1:T(8,128)(2,1)}, bf16[256,1024]{0,1:T(8,128)(2,1)}, u32[]{:S(2)}, u32[]{:S(2)}) collective-permute-start(bf16[256,1024]{0,1:T(8,128)(2,1)} %bitcast.11), channel_id=1, source_target_pairs={{0,4},{4,0},{8,12},{12,8},{16,20},{20,16},{24,28},{28,24},{1,5},{5... | collective-permute-start | bytes 1572872 | tf_op jit(solution)/shard_map/ppermute | solution.py:33
  37.2 27.6 %collective-permute-start = (bf16[64,1024]{1,0:T(8,128)(2,1)}, bf16[64,1024]{1,0:T(8,128)(2,1)}, u32[]{:S(2)}, u32[]{:S(2)}) collective-permute-start(bf16[64,1024]{1,0:T(8,128)(2,1)} %get-tuple-element.100), channel_id=1, source_target_pairs={{0,1},{1,2},{2,3},{3,0},{4,5},{5,6},{6,7},{7,4},{8,9},{9,10},{10,1... | collective-permute-start | bytes 393224 | tf_op jit(solution)/shard_map/ppermute | solution.py:37
  96.8 34.2 %collective-permute-start.40 = (bf16[256,2048]{1,0:T(8,128)(2,1)}, bf16[256,2048]{1,0:T(8,128)(2,1)S(1)}, u32[]{:S(2)}, u32[]{:S(2)}) collective-permute-start(bf16[256,2048]{1,0:T(8,128)(2,1)} %get-tuple-element.22), channel_id=1, source_target_pairs={{0,4},{4,0},{8,12},{12,8},{16,20},{20,16},{24,28},{28,24},{1,5},{5... | collective-permute-start | bytes 3145736 | tf_op jit(solution)/shard_map/ppermute | solution.py:33
  106.4 24.5 %collective-permute-start.43 = (bf16[256,2048]{1,0:T(8,128)(2,1)S(1)}, bf16[256,2048]{1,0:T(8,128)(2,1)S(1)}, u32[]{:S(2)}, u32[]{:S(2)}) collective-permute-start(bf16[256,2048]{1,0:T(8,128)(2,1)S(1)} %copy-done.21), channel_id=1, source_target_pairs={{0,16},{4,20},{8,24},{12,28},{16,0},{20,4},{24,8},{28,12},{1,17},{... | collective-permute-start | bytes 3145736 | tf_op jit(solution)/shard_map/ppermute | solution.py:33
  111.7 23.8 %collective-permute-start.41 = (bf16[256,2048]{1,0:T(8,128)(2,1)S(1)}, bf16[256,2048]{1,0:T(8,128)(2,1)S(1)}, u32[]{:S(2)}, u32[]{:S(2)}) collective-permute-start(bf16[256,2048]{1,0:T(8,128)(2,1)S(1)} %copy-done.21), channel_id=1, source_target_pairs={{0,8},{4,12},{8,0},{12,4},{16,24},{20,28},{24,16},{28,20},{1,9},{5... | collective-permute-start | bytes 3145736 | tf_op jit(solution)/shard_map/ppermute | solution.py:33
  130.9 43.6 %collective-permute-start.8 = (bf16[256,2048]{1,0:T(8,128)(2,1)S(1)}, bf16[256,2048]{1,0:T(8,128)(2,1)S(1)}, u32[]{:S(2)}, u32[]{:S(2)}) collective-permute-start(bf16[256,2048]{1,0:T(8,128)(2,1)S(1)} %pad_maximum_fusion.2), channel_id=1, source_target_pairs={{0,4},{4,0},{8,12},{12,8},{16,20},{20,16},{24,28},{28,24},{1,5},{5... | collective-permute-start | bytes 3145736 | tf_op jit(solution)/shard_map/ppermute | solution.py:33
  135.5 37.2 %collective-permute-start.9 = (bf16[256,2048]{1,0:T(8,128)(2,1)S(1)}, bf16[256,2048]{1,0:T(8,128)(2,1)S(1)}, u32[]{:S(2)}, u32[]{:S(2)}) collective-permute-start(bf16[256,2048]{1,0:T(8,128)(2,1)S(1)} %pad_maximum_fusion.2), channel_id=1, source_target_pairs={{0,8},{4,12},{8,0},{12,4},{16,24},{20,28},{24,16},{28,20},{1,9},{5... | collective-permute-start | bytes 3145736 | tf_op jit(solution)/shard_map/ppermute | solution.py:33
  137.1 35.5 %collective-permute-start.11 = (bf16[256,2048]{1,0:T(8,128)(2,1)S(1)}, bf16[256,2048]{1,0:T(8,128)(2,1)S(1)}, u32[]{:S(2)}, u32[]{:S(2)}) collective-permute-start(bf16[256,2048]{1,0:T(8,128)(2,1)S(1)} %pad_maximum_fusion.2), channel_id=1, source_target_pairs={{0,16},{4,20},{8,24},{12,28},{16,0},{20,4},{24,8},{28,12},{1,17},{... | collective-permute-start | bytes 3145736 | tf_op jit(solution)/shard_map/ppermute | solution.py:33
  138.7 30.9 %collective-permute-start.45 = (bf16[128,2048]{1,0:T(8,128)(2,1)S(1)}, bf16[128,2048]{1,0:T(8,128)(2,1)S(1)}, u32[]{:S(2)}, u32[]{:S(2)}) collective-permute-start(bf16[128,2048]{1,0:T(8,128)(2,1)S(1)} %slice.463), channel_id=1, source_target_pairs={{0,8},{4,12},{8,0},{12,4},{16,24},{20,28},{24,16},{28,20},{1,9},{5... | collective-permute-start | bytes 1572872 | tf_op jit(solution)/shard_map/ppermute | solution.py:33
  141.2 30.8 %collective-permute-start.46 = (bf16[128,2048]{1,0:T(8,128)(2,1)S(1)}, bf16[128,2048]{1,0:T(8,128)(2,1)S(1)}, u32[]{:S(2)}, u32[]{:S(2)}) collective-permute-start(bf16[128,2048]{1,0:T(8,128)(2,1)S(1)} %slice.464), channel_id=1, source_target_pairs={{0,16},{4,20},{8,24},{12,28},{16,0},{20,4},{24,8},{28,12},{1,17},{... | collective-permute-start | bytes 1572872 | tf_op jit(solution)/shard_map/ppermute | solution.py:33
  176.4 22.6 %collective-permute-start.10 = (bf16[256,2048]{1,0:T(8,128)(2,1)S(1)}, bf16[256,2048]{1,0:T(8,128)(2,1)S(1)}, u32[]{:S(2)}, u32[]{:S(2)}) collective-permute-start(bf16[256,2048]{1,0:T(8,128)(2,1)S(1)} %collective-permute-done.9), channel_id=1, source_target_pairs={{0,4},{4,0},{8,12},{12,8},{16,20},{20,16},{24,28},{28,24},{1,5},{5... | collective-permute-start | bytes 3145736 | tf_op jit(solution)/shard_map/ppermute | solution.py:33
  276.2 28.0 %collective-permute-start.49 = (bf16[256,2176]{1,0:T(8,128)(2,1)}, bf16[256,2176]{1,0:T(8,128)(2,1)S(1)}, u32[]{:S(2)}, u32[]{:S(2)}) collective-permute-start(bf16[256,2176]{1,0:T(8,128)(2,1)} %get-tuple-element.39), channel_id=1, source_target_pairs={{0,4},{4,0},{8,12},{12,8},{16,20},{20,16},{24,28},{28,24},{1,5},{5... | collective-permute-start | bytes 3342344 | tf_op jit(solution)/shard_map/ppermute | solution.py:33
  276.7 28.1 %collective-permute-start.53 = (bf16[256,2176]{1,0:T(8,128)(2,1)}, bf16[256,2176]{1,0:T(8,128)(2,1)}, u32[]{:S(2)}, u32[]{:S(2)}) collective-permute-start(bf16[256,2176]{1,0:T(8,128)(2,1)} %get-tuple-element.37), channel_id=1, source_target_pairs={{0,4},{4,0},{8,12},{12,8},{16,20},{20,16},{24,28},{28,24},{1,5},{5... | collective-permute-start | bytes 3342344 | tf_op jit(solution)/shard_map/ppermute | solution.py:33
  299.0 60.3 %collective-permute-start.48 = (bf16[256,2176]{1,0:T(8,128)(2,1)}, bf16[256,2176]{1,0:T(8,128)(2,1)}, u32[]{:S(2)}, u32[]{:S(2)}) collective-permute-start(bf16[256,2176]{1,0:T(8,128)(2,1)} %get-tuple-element.36), channel_id=1, source_target_pairs={{0,4},{4,0},{8,12},{12,8},{16,20},{20,16},{24,28},{28,24},{1,5},{5... | collective-permute-start | bytes 3342344 | tf_op jit(solution)/shard_map/ppermute | solution.py:33
  300.4 36.3 %collective-permute-start.24 = (bf16[256,2048]{1,0:T(8,128)(2,1)}, bf16[256,2048]{1,0:T(8,128)(2,1)}, u32[]{:S(2)}, u32[]{:S(2)}) collective-permute-start(bf16[256,2048]{1,0:T(8,128)(2,1)} %get-tuple-element.43), channel_id=1, source_target_pairs={{0,4},{4,0},{8,12},{12,8},{16,20},{20,16},{24,28},{28,24},{1,5},{5... | collective-permute-start | bytes 3145736 | tf_op jit(solution)/shard_map/ppermute | solution.py:33
  309.4 21.3 %collective-permute-start.54 = (bf16[128,2176]{1,0:T(8,128)(2,1)S(1)}, bf16[128,2176]{1,0:T(8,128)(2,1)S(1)}, u32[]{:S(2)}, u32[]{:S(2)}) collective-permute-start(bf16[128,2176]{1,0:T(8,128)(2,1)S(1)} %get-tuple-element.67), channel_id=1, source_target_pairs={{0,8},{4,12},{8,0},{12,4},{16,24},{20,28},{24,16},{28,20},{1,9},{5... | collective-permute-start | bytes 1671176 | tf_op jit(solution)/shard_map/ppermute | solution.py:33
  322.3 35.0 %collective-permute-start.31 = (bf16[256,2048]{1,0:T(8,128)(2,1)S(1)}, bf16[256,2048]{1,0:T(8,128)(2,1)S(1)}, u32[]{:S(2)}, u32[]{:S(2)}) collective-permute-start(bf16[256,2048]{1,0:T(8,128)(2,1)S(1)} %pad_maximum_fusion.5), channel_id=1, source_target_pairs={{0,16},{4,20},{8,24},{12,28},{16,0},{20,4},{24,8},{28,12},{1,17},{... | collective-permute-start | bytes 3145736 | tf_op jit(solution)/shard_map/ppermute | solution.py:33
  330.7 26.7 %collective-permute-start.28 = (bf16[256,2048]{1,0:T(8,128)(2,1)S(1)}, bf16[256,2048]{1,0:T(8,128)(2,1)S(1)}, u32[]{:S(2)}, u32[]{:S(2)}) collective-permute-start(bf16[256,2048]{1,0:T(8,128)(2,1)S(1)} %pad_maximum_fusion.4), channel_id=1, source_target_pairs={{0,8},{4,12},{8,0},{12,4},{16,24},{20,28},{24,16},{28,20},{1,9},{5... | collective-permute-start | bytes 3145736 | tf_op jit(solution)/shard_map/ppermute | solution.py:33
  334.9 44.4 %collective-permute-start.55 = (bf16[256,2176]{1,0:T(8,128)(2,1)S(1)}, bf16[256,2176]{1,0:T(8,128)(2,1)S(1)}, u32[]{:S(2)}, u32[]{:S(2)}) collective-permute-start(bf16[256,2176]{1,0:T(8,128)(2,1)S(1)} %pad_maximum_fusion.1), channel_id=1, source_target_pairs={{0,16},{4,20},{8,24},{12,28},{16,0},{20,4},{24,8},{28,12},{1,17},{... | collective-permute-start | bytes 3342344 | tf_op jit(solution)/shard_map/ppermute | solution.py:33
  336.7 42.6 %collective-permute-start.52 = (bf16[256,2176]{1,0:T(8,128)(2,1)S(1)}, bf16[256,2176]{1,0:T(8,128)(2,1)S(1)}, u32[]{:S(2)}, u32[]{:S(2)}) collective-permute-start(bf16[256,2176]{1,0:T(8,128)(2,1)S(1)} %pad_maximum_fusion), channel_id=1, source_target_pairs={{0,8},{4,12},{8,0},{12,4},{16,24},{20,28},{24,16},{28,20},{1,9},{5... | collective-permute-start | bytes 3342344 | tf_op jit(solution)/shard_map/ppermute | solution.py:33
  415.8 113.6 %collective-permute-start.35 = (bf16[64,2048]{1,0:T(8,128)(2,1)}, bf16[64,2048]{1,0:T(8,128)(2,1)}, u32[]{:S(2)}, u32[]{:S(2)}) collective-permute-start(bf16[64,2048]{1,0:T(8,128)(2,1)} %pad_maximum_fusion.18), channel_id=1, source_target_pairs={{0,3},{1,0},{2,1},{3,2},{4,7},{5,4},{6,5},{7,6},{8,11},{9,8},{10,9... | collective-permute-start | bytes 786440 | tf_op jit(solution)/shard_map/ppermute | solution.py:37
  424.7 44.8 %collective-permute-start.63 = (bf16[64,1024]{1,0:T(8,128)(2,1)S(1)}, bf16[64,1024]{1,0:T(8,128)(2,1)S(1)}, u32[]{:S(2)}, u32[]{:S(2)}) collective-permute-start(bf16[64,1024]{1,0:T(8,128)(2,1)S(1)} %slice.490), channel_id=1, source_target_pairs={{0,3},{1,0},{2,1},{3,2},{4,7},{5,4},{6,5},{7,6},{8,11},{9,8},{10,9... | collective-permute-start | bytes 393224 | tf_op jit(solution)/shard_map/ppermute | solution.py:37
  428.1 41.4 %collective-permute-start.62 = (bf16[64,1024]{1,0:T(8,128)(2,1)S(1)}, bf16[64,1024]{1,0:T(8,128)(2,1)S(1)}, u32[]{:S(2)}, u32[]{:S(2)}) collective-permute-start(bf16[64,1024]{1,0:T(8,128)(2,1)S(1)} %slice.489), channel_id=1, source_target_pairs={{0,1},{1,2},{2,3},{3,0},{4,5},{5,6},{6,7},{7,4},{8,9},{9,10},{10,1... | collective-permute-start | bytes 393224 | tf_op jit(solution)/shard_map/ppermute | solution.py:37
  516.7 87.3 %collective-permute-start.79 = (bf16[256,1280]{1,0:T(8,128)(2,1)}, bf16[256,1280]{1,0:T(8,128)(2,1)}, u32[]{:S(2)}, u32[]{:S(2)}) collective-permute-start(bf16[256,1280]{1,0:T(8,128)(2,1)} %get-tuple-element.104), channel_id=1, source_target_pairs={{0,4},{4,0},{8,12},{12,8},{16,20},{20,16},{24,28},{28,24},{1,5},{5... | collective-permute-start | bytes 1966088 | tf_op jit(solution)/shard_map/ppermute | solution.py:33
  521.8 77.1 %collective-permute-start.80 = (bf16[256,1280]{1,0:T(8,128)(2,1)}, bf16[256,1280]{1,0:T(8,128)(2,1)}, u32[]{:S(2)}, u32[]{:S(2)}) collective-permute-start(bf16[256,1280]{1,0:T(8,128)(2,1)} %get-tuple-element.104), channel_id=1, source_target_pairs={{0,8},{4,12},{8,0},{12,4},{16,24},{20,28},{24,16},{28,20},{1,9},{5... | collective-permute-start | bytes 1966088 | tf_op jit(solution)/shard_map/ppermute | solution.py:33
  527.4 70.4 %collective-permute-start.82 = (bf16[256,1280]{1,0:T(8,128)(2,1)}, bf16[256,1280]{1,0:T(8,128)(2,1)}, u32[]{:S(2)}, u32[]{:S(2)}) collective-permute-start(bf16[256,1280]{1,0:T(8,128)(2,1)} %get-tuple-element.104), channel_id=1, source_target_pairs={{0,16},{4,20},{8,24},{12,28},{16,0},{20,4},{24,8},{28,12},{1,17},{... | collective-permute-start | bytes 1966088 | tf_op jit(solution)/shard_map/ppermute | solution.py:33
  534.3 44.3 %collective-permute-start.36 = (bf16[64,2048]{1,0:T(8,128)(2,1)}, bf16[64,2048]{1,0:T(8,128)(2,1)S(1)}, u32[]{:S(2)}, u32[]{:S(2)}) collective-permute-start(bf16[64,2048]{1,0:T(8,128)(2,1)} %get-tuple-element.107), channel_id=1, source_target_pairs={{0,3},{1,0},{2,1},{3,2},{4,7},{5,4},{6,5},{7,6},{8,11},{9,8},{10,9... | collective-permute-start | bytes 786440 | tf_op jit(solution)/shard_map/ppermute | solution.py:37
  537.0 43.2 %collective-permute-start.37 = (bf16[64,2048]{1,0:T(8,128)(2,1)}, bf16[64,2048]{1,0:T(8,128)(2,1)S(1)}, u32[]{:S(2)}, u32[]{:S(2)}) collective-permute-start(bf16[64,2048]{1,0:T(8,128)(2,1)} %get-tuple-element.107), channel_id=1, source_target_pairs={{0,1},{1,2},{2,3},{3,0},{4,5},{5,6},{6,7},{7,4},{8,9},{9,10},{10,1... | collective-permute-start | bytes 786440 | tf_op jit(solution)/shard_map/ppermute | solution.py:37
  (189 other events, 2418.6 us)
Sparse Core Ops, SparseCore 0:
  416.9 32.4 reduce-scatter.1
where the time goes:
time: 648 us; the launch traced here: 638 us
  waiting for transfers between devices  165 us (25%)
  matrix products  139 us (21%)
  starting transfers between devices  110 us (17%)
  local copies, waits for them, and re-layouts  83.2 us (13%)
  other arithmetic  65 us (10%)
  blocking collectives  58.9 us (9%)
  between operations  16.9 us (3%)
    ppermute x70, waiting for transfers between devices, swap(): return lax.ppermute(value, 'dp', [(i, i ^ bit) for i in range(count)])  104 us
    ppermute x32, starting transfers between devices, shift(): lax.ppermute(value, 'tensor', [(i, (i + step) % count) for i in range(cou...  56.7 us
    unnamed x290, local copies, waits for them, and re-layouts  53.5 us
    ppermute x70, starting transfers between devices, swap(): return lax.ppermute(value, 'dp', [(i, i ^ bit) for i in range(count)])  53.5 us
    ppermute x32, waiting for transfers between devices, shift(): lax.ppermute(value, 'tensor', [(i, (i + step) % count) for i in range(cou...  44.8 us
    dot_general x9, matrix products, dot_nn(): lax.dot_general(a, b, (((1,), (0,)), ((), ())), preferred_element_type=F32)  42.5 us
    psum x1, blocking collectives, local(): gains = lax.psum(gains, ('dp', 'tensor'))  39.3 us
    dot_general x6, matrix products, dot_tn(): lax.dot_general(a, b, (((0,), (0,)), ((), ())), preferred_element_type=F32)  37.1 us
  transfers between devices with their start and end apart: 103, of which 31 were waited for; matrix products, arithmetic and copies ran while one was open for 30% of the time, Pallas kernels for 0%

commit v1 on v0

--- a/solution.py
+++ b/solution.py
@@ -316,8 +316,12 @@
     query_weight_grad = qkv_w[:, :q_cols]
     key_weight_grad = qkv_w[:, q_cols : q_cols + kv_cols]
     value_weight_grad = qkv_w[:, q_cols + kv_cols :]
-    router_sum = lax.psum(
-        lax.psum_scatter(router_part.astype(BF16), "dp", scatter_dimension=0, tiled=True), "tensor"
+    router_sum = jnp.sum(
+        lax.all_gather(
+            lax.psum_scatter(router_part.astype(BF16), "dp", scatter_dimension=0, tiled=True),
+            "tensor",
+        ),
+        axis=0,
     ).astype(F32)
     gains = jnp.concatenate([attn_gain_part, ffn_gain_part, q_gain_part, k_gain_part])
     gains = lax.psum(gains, ("dp", "tensor"))

time: 648 us -> 642 us (level)
    psum x1 -> x0, blocking collectives: 19.5 us -> none  [local(): lax.psum(lax.psum_scatter(router_part.astype(BF16), 'dp', scatter_dimensi...]
    all_gather x0 -> x1, blocking collectives: none -> 13.5 us  [local(): lax.all_gather(lax.psum_scatter(router_part.astype(BF16), 'dp', scatter_d...]
  transfers between devices with their start and end apart: 103 -> 103, of which waited for: 31 -> 32; matrix products, arithmetic and copies ran while one was open for 30% -> 30% of each run, Pallas kernels for 0% -> 0%
where the time goes in v1:
time: 642 us; the launch traced here: 632 us
  waiting for transfers between devices  165 us (26%)
  matrix products  139 us (22%)
  starting transfers between devices  110 us (17%)
  local copies, waits for them, and re-layouts  83.2 us (13%)
  other arithmetic  64.9 us (10%)
  blocking collectives  52.6 us (8%)
  between operations  16.9 us (3%)
    ppermute x70, waiting for transfers between devices, swap(): return lax.ppermute(value, 'dp', [(i, i ^ bit) for i in range(count)])  108 us
    ppermute x70, starting transfers between devices, swap(): return lax.ppermute(value, 'dp', [(i, i ^ bit) for i in range(count)])  57.7 us
    unnamed x290, local copies, waits for them, and re-layouts  53.6 us
    ppermute x32, starting transfers between devices, shift(): lax.ppermute(value, 'tensor', [(i, (i + step) % count) for i in range(cou...  52 us
    dot_general x9, matrix products, dot_nn(): lax.dot_general(a, b, (((1,), (0,)), ((), ())), preferred_element_type=F32)  42.5 us
    ppermute x32, waiting for transfers between devices, shift(): lax.ppermute(value, 'tensor', [(i, (i + step) % count) for i in range(cou...  41 us
    psum x1, blocking collectives, local(): gains = lax.psum(gains, ('dp', 'tensor'))  39 us
    dot_general x6, matrix products, dot_tn(): lax.dot_general(a, b, (((0,), (0,)), ((), ())), preferred_element_type=F32)  37.1 us
  transfers between devices with their start and end apart: 103, of which 32 were waited for; matrix products, arithmetic and copies ran while one was open for 30% of the time, Pallas kernels for 0%

profile of v1, /device:TPU:0, one launch (start us, length us, event | category | flops | bytes accessed | tf_op | source)
XLA Modules:
  0.0 631.6 jit_solution(1307401260524298161)
XLA Ops:
  75.1 4.1 collective-permute-done.76
  83.7 6.4 %collective-permute-done.1 = bf16[64,2048]{1,0:T(8,128)(2,1)S(1)} collective-permute-done((bf16[64,2048]{1,0:T(8,128)(2,1)S(1)}, bf16[64,2048]{1,0:T(8,128)(2,1)S(1)}, u32[]{:S(2)}, u32[]{:S(2)}) %collective-permute-start.1) | collective-permute-done | bytes 262176 | tf_op jit(solution)/shard_map/ppermute | solution.py:37
  121.8 9.1 %collective-permute-done.43 = bf16[256,2048]{1,0:T(8,128)(2,1)S(1)} collective-permute-done((bf16[256,2048]{1,0:T(8,128)(2,1)S(1)}, bf16[256,2048]{1,0:T(8,128)(2,1)S(1)}, u32[]{:S(2)}, u32[]{:S(2)}) %collective-permute-start.43) | collective-permute-done | bytes 1048608 | tf_op jit(solution)/shard_map/ppermute | solution.py:33
  144.5 25.2 %collective-permute-done.45 = bf16[128,2048]{1,0:T(8,128)(2,1)S(1)} collective-permute-done((bf16[128,2048]{1,0:T(8,128)(2,1)S(1)}, bf16[128,2048]{1,0:T(8,128)(2,1)S(1)}, u32[]{:S(2)}, u32[]{:S(2)}) %collective-permute-start.45) | collective-permute-done | bytes 524320 | tf_op jit(solution)/shard_map/ppermute | solution.py:33
  181.9 5.3 collective-permute-done.13
  189.9 9.1 %fusion.111 = f32[2048,768]{1,0:T(8,128)S(1)} fusion(bf16[2048,2048]{1,0:T(8,128)(2,1)} %constant_dynamic-update-slice_fusion.21, bf16[768,2048]{1,0:T(8,128)(2,1)S(1)} %bitcast.213), kind=kOutput, calls=%fused_computation.348 | convolution fusion | flops 6442450944 | bytes 17825792 | tf_op jit(solution)/shard_map/dot_general | solution.py:25
  204.4 8.6 %fusion.110 = f32[2048,768]{1,0:T(8,128)} fusion(bf16[2048,2048]{1,0:T(8,128)(2,1)S(1)} %constant_dynamic-update-slice_fusion, bf16[768,2048]{1,0:T(8,128)(2,1)S(1)} %bitcast.211), kind=kOutput, calls=%fused_computation.347 | convolution fusion | flops 6442450944 | bytes 17825792 | tf_op jit(solution)/shard_map/dot_general | solution.py:25
  213.0 8.6 %fusion.109 = f32[2048,768]{1,0:T(8,128)} fusion(bf16[2048,2048]{1,0:T(8,128)(2,1)S(1)} %constant_dynamic-update-slice_fusion, bf16[768,2048]{1,0:T(8,128)(2,1)S(1)} %bitcast.194), kind=kOutput, calls=%fused_computation.346 | convolution fusion | flops 6442450944 | bytes 17825792 | tf_op jit(solution)/shard_map/dot_general | solution.py:25
  221.6 7.6 %fusion.7 = bf16[2048,32]{0,1:T(8,128)(2,1)} fusion(f32[2048,768]{1,0:T(8,128)S(1)} %fusion.111, f32[2048,768]{1,0:T(8,128)S(1)} %copy-done.106, s32[768]{0:T(1024)S(1)} %fusion.79, f32[2048,768]{1,0:T(8,128)} %fusion.109), kind=kOutput, calls=%fused_computation.17 | convolution fusion | flops 613507072 | bytes 19008512 | tf_op jit(solution)/shard_map/dot_general | solution.py:235
  231.2 10.7 %multiply_convert_fusion = (bf16[2048,768]{1,0:T(8,128)(2,1)S(1)}, bf16[2048,768]{1,0:T(8,128)(2,1)S(1)}, bf16[2048,768]{1,0:T(8,128)(2,1)}) fusion(f32[2048,768]{1,0:T(8,128)} %copy-done.105, f32[2048,768]{1,0:T(8,128)} %fusion.109, f32[2048,768]{1,0:T(8,128)} %fusion.110, s32[768]{0:T(1024)S(1)} %fusion.79, f32[2048]{0:T(1024)S(1)} %fusion.76, ...), kind=kOutput, calls=%fused_computation.7 | convolution fusion | flops 631005184 | bytes 28666880 | tf_op jit(solution)/shard_map/dot_general | solution.py:224
  242.0 9.5 %fusion.112 = f32[2048,2048]{1,0:T(8,128)} fusion(bf16[2048,768]{1,0:T(8,128)(2,1)S(1)} %get-tuple-element.34, bf16[768,2048]{1,0:T(8,128)(2,1)S(1)} %bitcast.195), kind=kOutput, calls=%fused_computation.349 | convolution fusion | flops 6442450944 | bytes 23068672 | tf_op jit(solution)/shard_map/dot_general | solution.py:21
  251.5 12.6 %add_convert_fusion = bf16[2048,2048]{1,0:T(8,128)(2,1)} fusion(f32[2048,2048]{1,0:T(8,128)} %fusion.112, bf16[2048,768]{1,0:T(8,128)(2,1)S(1)} %get-tuple-element.33, bf16[768,2048]{1,0:T(8,128)(2,1)S(1)} %bitcast.212), kind=kOutput, calls=%fused_computation.2 | convolution fusion | flops 6450839552 | bytes 31457280 | tf_op jit(solution)/shard_map/dot_general | solution.py:21
  264.0 8.0 %fusion.1 = bf16[2048,2176]{1,0:T(8,128)(2,1)} fusion(bf16[2048,32]{1,0:T(8,128)(2,1)S(1)} %copy-done.26, bf16[2048,2048]{1,0:T(8,128)(2,1)} %add_convert_fusion), kind=kLoop, calls=%fused_computation.3 | loop fusion | flops 26738688 | bytes 17432576 | tf_op jit(solution)/shard_map/concatenate | solution.py:243
  272.0 4.2 fusion.94
  276.7 9.2 %convolution_convert_fusion = bf16[2048,2048]{1,0:T(8,128)(2,1)S(1)} fusion(bf16[2048,768]{1,0:T(8,128)(2,1)} %get-tuple-element.35, bf16[768,2048]{1,0:T(8,128)(2,1)S(1)} %bitcast.214), kind=kOutput, calls=%fused_computation.4 | convolution fusion | flops 6446645248 | bytes 14680064 | tf_op jit(solution)/shard_map/dot_general | solution.py:21
  288.4 10.5 %fusion.116 = f32[768,2048]{1,0:T(8,128)} fusion(bf16[2048,768]{1,0:T(8,128)(2,1)} %copy-done.109, bf16[2048,2048]{1,0:T(8,128)(2,1)S(1)} %bitcast.202), kind=kOutput, calls=%fused_computation.353 | convolution fusion | flops 6442450944 | bytes 17825792 | tf_op jit(solution)/shard_map/dot_general | solution.py:29
  310.9 8.4 %collective-permute-done.30 = bf16[128,2048]{1,0:T(8,128)(2,1)} collective-permute-done((bf16[128,2048]{1,0:T(8,128)(2,1)}, bf16[128,2048]{1,0:T(8,128)(2,1)}, u32[]{:S(2)}, u32[]{:S(2)}) %collective-permute-start.30) | collective-permute-done | bytes 524320 | tf_op jit(solution)/shard_map/ppermute | solution.py:33
  323.0 7.7 %collective-permute-done.54 = bf16[128,2176]{1,0:T(8,128)(2,1)S(1)} collective-permute-done((bf16[128,2176]{1,0:T(8,128)(2,1)S(1)}, bf16[128,2176]{1,0:T(8,128)(2,1)S(1)}, u32[]{:S(2)}, u32[]{:S(2)}) %collective-permute-start.54) | collective-permute-done | bytes 557088 | tf_op jit(solution)/shard_map/ppermute | solution.py:33
  337.4 10.7 %fusion.117 = f32[768,2048]{1,0:T(8,128)} fusion(bf16[2048,768]{1,0:T(8,128)(2,1)} %copy-done.108, bf16[2048,2048]{1,0:T(8,128)(2,1)S(1)} %bitcast.202), kind=kOutput, calls=%fused_computation.354 | convolution fusion | flops 6442450944 | bytes 17825792 | tf_op jit(solution)/shard_map/dot_general | solution.py:29
  348.1 9.2 %collective-permute-done.31 = bf16[256,2048]{1,0:T(8,128)(2,1)S(1)} collective-permute-done((bf16[256,2048]{1,0:T(8,128)(2,1)S(1)}, bf16[256,2048]{1,0:T(8,128)(2,1)S(1)}, u32[]{:S(2)}, u32[]{:S(2)}) %collective-permute-start.31) | collective-permute-done | bytes 1048608 | tf_op jit(solution)/shard_map/ppermute | solution.py:33
  359.3 20.0 %collective-permute-done.55 = bf16[256,2176]{1,0:T(8,128)(2,1)S(1)} collective-permute-done((bf16[256,2176]{1,0:T(8,128)(2,1)S(1)}, bf16[256,2176]{1,0:T(8,128)(2,1)S(1)}, u32[]{:S(2)}, u32[]{:S(2)}) %collective-permute-start.55) | collective-permute-done | bytes 1114144 | tf_op jit(solution)/shard_map/ppermute | solution.py:33
  395.1 11.0 %fusion.118 = f32[768,2048]{1,0:T(8,128)} fusion(bf16[2048,768]{1,0:T(8,128)(2,1)S(1)} %copy-done.107, bf16[2048,2048]{1,0:T(8,128)(2,1)} %constant_dynamic-update-slice_fusion.21), kind=kOutput, calls=%fused_computation.355 | convolution fusion | flops 6442450944 | bytes 17825792 | tf_op jit(solution)/shard_map/dot_general | solution.py:29
  416.8 7.9 %collective-permute-done.60 = bf16[64,2048]{1,0:T(8,128)(2,1)S(1)} collective-permute-done((bf16[64,2048]{1,0:T(8,128)(2,1)S(1)}, bf16[64,2048]{1,0:T(8,128)(2,1)S(1)}, u32[]{:S(2)}, u32[]{:S(2)}) %collective-permute-start.60) | collective-permute-done | bytes 262176 | tf_op jit(solution)/shard_map/ppermute | solution.py:37
  428.1 4.8 collective-permute-start.62
  433.6 15.8 %reduce-scatter.2.cloned.1.call-done = bf16[256,32]{0,1:T(8,128)(2,1)} async-done(((bf16[2048,32]{0,1:T(8,128)(2,1)}), bf16[256,32]{0,1:T(8,128)(2,1)}) %reduce-scatter.2.cloned.1.call-update) | async-done | bytes 16400 | tf_op jit(solution)/shard_map/reduce_scatter | solution.py:321
  449.4 13.5 %all-gather = bf16[1024,32]{0,1:T(8,128)(2,1)S(1)} all-gather(bf16[256,32]{0,1:T(8,128)(2,1)} %reduce-scatter.2.cloned.1.call-done), channel_id=2, replica_groups=mesh['dp'=8,'tensor'=4] {'tensor'}, dimensions={0}, use_global_device_ids=true | all-gather | bytes 81920 | tf_op jit(solution)/shard_map/all_gather | solution.py:320
  505.2 5.1 collective-permute-done.91
  511.9 7.1 %collective-permute-start.80 = (bf16[256,1280]{1,0:T(8,128)(2,1)}, bf16[256,1280]{1,0:T(8,128)(2,1)}, u32[]{:S(2)}, u32[]{:S(2)}) collective-permute-start(bf16[256,1280]{1,0:T(8,128)(2,1)} %get-tuple-element.104), channel_id=1, source_target_pairs={{0,8},{4,12},{8,0},{12,4},{16,24},{20,28},{24,16},{28,20},{1,9},{5... | collective-permute-start | bytes 1966088 | tf_op jit(solution)/shard_map/ppermute | solution.py:33
  533.1 39.0 %psum.7 = f32[4352]{0:T(1024)S(1)} all-reduce(f32[4352]{0:T(1024)S(1)} %pad_maximum_fusion.24), channel_id=1, replica_groups=mesh['dp'=8,'tensor'=4] {'dp','tensor'}, use_global_device_ids=true, to_apply=%region_27.29 | all-reduce | flops 4352 | bytes 34816 | tf_op jit(solution)/shard_map/psum | solution.py:327
  576.9 10.7 %collective-permute-done.69 = bf16[64,2048]{1,0:T(8,128)(2,1)S(1)} collective-permute-done((bf16[64,2048]{1,0:T(8,128)(2,1)S(1)}, bf16[64,2048]{1,0:T(8,128)(2,1)S(1)}, u32[]{:S(2)}, u32[]{:S(2)}) %collective-permute-start.69) | collective-permute-done | bytes 262176 | tf_op jit(solution)/shard_map/ppermute | solution.py:37
  604.4 7.4 %fusion.33 = bf16[256,2048]{1,0:T(8,128)(2,1)} fusion(s32[]{:T(128)S(6)} %select_n.114, bf16[64,2048]{1,0:T(8,128)(2,1)} %get-tuple-element.107, bf16[64,2048]{1,0:T(8,128)(2,1)S(1)} %collective-permute-done.36, bf16[64,1024]{1,0:T(8,128)(2,1)S(1)} %collective-permute-done.38, bf16[64,1024]{1,0:T(8,128)(2,1)S(1)} %collective-permute-done.39, ...), kind=kLoop, calls=%fused_computation.92 | loop fusion | flops 10485760 | bytes 2097156 | tf_op jit(solution)/shard_map/jit(_roll_dynamic)/concatenate | solution.py:109
  612.2 6.5 %fusion.23 = bf16[256,2048]{1,0:T(8,128)(2,1)} fusion(s32[]{:T(128)S(6)} %select_n.114, bf16[64,2048]{1,0:T(8,128)(2,1)S(1)} %get-tuple-element.106, bf16[64,2048]{1,0:T(8,128)(2,1)S(1)} %collective-permute-done.68, bf16[64,1024]{1,0:T(8,128)(2,1)S(1)} %collective-permute-done.70, bf16[64,1024]{1,0:T(8,128)(2,1)S(1)} %collective-permute-done.71, ...), kind=kLoop, calls=%fused_computation.82 | loop fusion | flops 10485760 | bytes 2097156 | tf_op jit(solution)/shard_map/jit(_roll_dynamic)/concatenate | solution.py:109
  (650 shorter events, 281.2 us)
Async XLA Ops:
  7.2 442.2 %reduce-scatter.2.cloned.1.call-start = ((), (), s32[]{:S(2)}) async-start(), calls=%async_computation.1 | async-start | bytes 147456 | tf_op jit(solution)/shard_map/reduce_scatter | solution.py:321
  8.8 44.6 %collective-permute-start.16 = (s32[256,8]{0,1:T(8,128)S(1)}, s32[256,8]{0,1:T(8,128)S(1)}, u32[]{:S(2)}, u32[]{:S(2)}) collective-permute-start(s32[256,8]{0,1:T(8,128)S(1)} %get-tuple-element.28), channel_id=1, source_target_pairs={{0,4},{4,0},{8,12},{12,8},{16,20},{20,16},{24,28},{28,24},{1,5},{5... | collective-permute-start | bytes 24584 | tf_op jit(solution)/shard_map/ppermute | solution.py:33
  9.3 43.6 %collective-permute-start.17 = (s32[256,8]{0,1:T(8,128)S(1)}, s32[256,8]{0,1:T(8,128)S(1)}, u32[]{:S(2)}, u32[]{:S(2)}) collective-permute-start(s32[256,8]{0,1:T(8,128)S(1)} %get-tuple-element.28), channel_id=1, source_target_pairs={{0,8},{4,12},{8,0},{12,4},{16,24},{20,28},{24,16},{28,20},{1,9},{5... | collective-permute-start | bytes 24584 | tf_op jit(solution)/shard_map/ppermute | solution.py:33
  11.8 38.7 %collective-permute-start.19 = (s32[256,8]{0,1:T(8,128)S(1)}, s32[256,8]{0,1:T(8,128)S(1)}, u32[]{:S(2)}, u32[]{:S(2)}) collective-permute-start(s32[256,8]{0,1:T(8,128)S(1)} %get-tuple-element.28), channel_id=1, source_target_pairs={{0,16},{4,20},{8,24},{12,28},{16,0},{20,4},{24,8},{28,12},{1,17},{... | collective-permute-start | bytes 24584 | tf_op jit(solution)/shard_map/ppermute | solution.py:33
  31.7 68.2 %collective-permute-start.94 = (bf16[256,1024]{0,1:T(8,128)(2,1)}, bf16[256,1024]{0,1:T(8,128)(2,1)}, u32[]{:S(2)}, u32[]{:S(2)}) collective-permute-start(bf16[256,1024]{0,1:T(8,128)(2,1)} %bitcast.11), channel_id=1, source_target_pairs={{0,4},{4,0},{8,12},{12,8},{16,20},{20,16},{24,28},{28,24},{1,5},{5... | collective-permute-start | bytes 1572872 | tf_op jit(solution)/shard_map/ppermute | solution.py:33
  37.2 27.6 %collective-permute-start = (bf16[64,1024]{1,0:T(8,128)(2,1)}, bf16[64,1024]{1,0:T(8,128)(2,1)}, u32[]{:S(2)}, u32[]{:S(2)}) collective-permute-start(bf16[64,1024]{1,0:T(8,128)(2,1)} %get-tuple-element.100), channel_id=1, source_target_pairs={{0,1},{1,2},{2,3},{3,0},{4,5},{5,6},{6,7},{7,4},{8,9},{9,10},{10,1... | collective-permute-start | bytes 393224 | tf_op jit(solution)/shard_map/ppermute | solution.py:37
  96.8 34.2 %collective-permute-start.40 = (bf16[256,2048]{1,0:T(8,128)(2,1)}, bf16[256,2048]{1,0:T(8,128)(2,1)S(1)}, u32[]{:S(2)}, u32[]{:S(2)}) collective-permute-start(bf16[256,2048]{1,0:T(8,128)(2,1)} %get-tuple-element.22), channel_id=1, source_target_pairs={{0,4},{4,0},{8,12},{12,8},{16,20},{20,16},{24,28},{28,24},{1,5},{5... | collective-permute-start | bytes 3145736 | tf_op jit(solution)/shard_map/ppermute | solution.py:33
  106.4 24.5 %collective-permute-start.43 = (bf16[256,2048]{1,0:T(8,128)(2,1)S(1)}, bf16[256,2048]{1,0:T(8,128)(2,1)S(1)}, u32[]{:S(2)}, u32[]{:S(2)}) collective-permute-start(bf16[256,2048]{1,0:T(8,128)(2,1)S(1)} %copy-done.21), channel_id=1, source_target_pairs={{0,16},{4,20},{8,24},{12,28},{16,0},{20,4},{24,8},{28,12},{1,17},{... | collective-permute-start | bytes 3145736 | tf_op jit(solution)/shard_map/ppermute | solution.py:33
  111.7 23.8 %collective-permute-start.41 = (bf16[256,2048]{1,0:T(8,128)(2,1)S(1)}, bf16[256,2048]{1,0:T(8,128)(2,1)S(1)}, u32[]{:S(2)}, u32[]{:S(2)}) collective-permute-start(bf16[256,2048]{1,0:T(8,128)(2,1)S(1)} %copy-done.21), channel_id=1, source_target_pairs={{0,8},{4,12},{8,0},{12,4},{16,24},{20,28},{24,16},{28,20},{1,9},{5... | collective-permute-start | bytes 3145736 | tf_op jit(solution)/shard_map/ppermute | solution.py:33
  130.9 43.6 %collective-permute-start.8 = (bf16[256,2048]{1,0:T(8,128)(2,1)S(1)}, bf16[256,2048]{1,0:T(8,128)(2,1)S(1)}, u32[]{:S(2)}, u32[]{:S(2)}) collective-permute-start(bf16[256,2048]{1,0:T(8,128)(2,1)S(1)} %pad_maximum_fusion.2), channel_id=1, source_target_pairs={{0,4},{4,0},{8,12},{12,8},{16,20},{20,16},{24,28},{28,24},{1,5},{5... | collective-permute-start | bytes 3145736 | tf_op jit(solution)/shard_map/ppermute | solution.py:33
  135.5 37.2 %collective-permute-start.9 = (bf16[256,2048]{1,0:T(8,128)(2,1)S(1)}, bf16[256,2048]{1,0:T(8,128)(2,1)S(1)}, u32[]{:S(2)}, u32[]{:S(2)}) collective-permute-start(bf16[256,2048]{1,0:T(8,128)(2,1)S(1)} %pad_maximum_fusion.2), channel_id=1, source_target_pairs={{0,8},{4,12},{8,0},{12,4},{16,24},{20,28},{24,16},{28,20},{1,9},{5... | collective-permute-start | bytes 3145736 | tf_op jit(solution)/shard_map/ppermute | solution.py:33
  137.1 35.5 %collective-permute-start.11 = (bf16[256,2048]{1,0:T(8,128)(2,1)S(1)}, bf16[256,2048]{1,0:T(8,128)(2,1)S(1)}, u32[]{:S(2)}, u32[]{:S(2)}) collective-permute-start(bf16[256,2048]{1,0:T(8,128)(2,1)S(1)} %pad_maximum_fusion.2), channel_id=1, source_target_pairs={{0,16},{4,20},{8,24},{12,28},{16,0},{20,4},{24,8},{28,12},{1,17},{... | collective-permute-start | bytes 3145736 | tf_op jit(solution)/shard_map/ppermute | solution.py:33
  138.7 30.9 %collective-permute-start.45 = (bf16[128,2048]{1,0:T(8,128)(2,1)S(1)}, bf16[128,2048]{1,0:T(8,128)(2,1)S(1)}, u32[]{:S(2)}, u32[]{:S(2)}) collective-permute-start(bf16[128,2048]{1,0:T(8,128)(2,1)S(1)} %slice.463), channel_id=1, source_target_pairs={{0,8},{4,12},{8,0},{12,4},{16,24},{20,28},{24,16},{28,20},{1,9},{5... | collective-permute-start | bytes 1572872 | tf_op jit(solution)/shard_map/ppermute | solution.py:33
  141.2 30.8 %collective-permute-start.46 = (bf16[128,2048]{1,0:T(8,128)(2,1)S(1)}, bf16[128,2048]{1,0:T(8,128)(2,1)S(1)}, u32[]{:S(2)}, u32[]{:S(2)}) collective-permute-start(bf16[128,2048]{1,0:T(8,128)(2,1)S(1)} %slice.464), channel_id=1, source_target_pairs={{0,16},{4,20},{8,24},{12,28},{16,0},{20,4},{24,8},{28,12},{1,17},{... | collective-permute-start | bytes 1572872 | tf_op jit(solution)/shard_map/ppermute | solution.py:33
  176.4 22.6 %collective-permute-start.10 = (bf16[256,2048]{1,0:T(8,128)(2,1)S(1)}, bf16[256,2048]{1,0:T(8,128)(2,1)S(1)}, u32[]{:S(2)}, u32[]{:S(2)}) collective-permute-start(bf16[256,2048]{1,0:T(8,128)(2,1)S(1)} %collective-permute-done.9), channel_id=1, source_target_pairs={{0,4},{4,0},{8,12},{12,8},{16,20},{20,16},{24,28},{28,24},{1,5},{5... | collective-permute-start | bytes 3145736 | tf_op jit(solution)/shard_map/ppermute | solution.py:33
  276.2 28.0 %collective-permute-start.49 = (bf16[256,2176]{1,0:T(8,128)(2,1)}, bf16[256,2176]{1,0:T(8,128)(2,1)S(1)}, u32[]{:S(2)}, u32[]{:S(2)}) collective-permute-start(bf16[256,2176]{1,0:T(8,128)(2,1)} %get-tuple-element.39), channel_id=1, source_target_pairs={{0,4},{4,0},{8,12},{12,8},{16,20},{20,16},{24,28},{28,24},{1,5},{5... | collective-permute-start | bytes 3342344 | tf_op jit(solution)/shard_map/ppermute | solution.py:33
  276.7 28.1 %collective-permute-start.53 = (bf16[256,2176]{1,0:T(8,128)(2,1)}, bf16[256,2176]{1,0:T(8,128)(2,1)}, u32[]{:S(2)}, u32[]{:S(2)}) collective-permute-start(bf16[256,2176]{1,0:T(8,128)(2,1)} %get-tuple-element.37), channel_id=1, source_target_pairs={{0,4},{4,0},{8,12},{12,8},{16,20},{20,16},{24,28},{28,24},{1,5},{5... | collective-permute-start | bytes 3342344 | tf_op jit(solution)/shard_map/ppermute | solution.py:33
  299.0 60.3 %collective-permute-start.48 = (bf16[256,2176]{1,0:T(8,128)(2,1)}, bf16[256,2176]{1,0:T(8,128)(2,1)}, u32[]{:S(2)}, u32[]{:S(2)}) collective-permute-start(bf16[256,2176]{1,0:T(8,128)(2,1)} %get-tuple-element.36), channel_id=1, source_target_pairs={{0,4},{4,0},{8,12},{12,8},{16,20},{20,16},{24,28},{28,24},{1,5},{5... | collective-permute-start | bytes 3342344 | tf_op jit(solution)/shard_map/ppermute | solution.py:33
  300.4 36.3 %collective-permute-start.24 = (bf16[256,2048]{1,0:T(8,128)(2,1)}, bf16[256,2048]{1,0:T(8,128)(2,1)}, u32[]{:S(2)}, u32[]{:S(2)}) collective-permute-start(bf16[256,2048]{1,0:T(8,128)(2,1)} %get-tuple-element.43), channel_id=1, source_target_pairs={{0,4},{4,0},{8,12},{12,8},{16,20},{20,16},{24,28},{28,24},{1,5},{5... | collective-permute-start | bytes 3145736 | tf_op jit(solution)/shard_map/ppermute | solution.py:33
  309.4 21.3 %collective-permute-start.54 = (bf16[128,2176]{1,0:T(8,128)(2,1)S(1)}, bf16[128,2176]{1,0:T(8,128)(2,1)S(1)}, u32[]{:S(2)}, u32[]{:S(2)}) collective-permute-start(bf16[128,2176]{1,0:T(8,128)(2,1)S(1)} %get-tuple-element.67), channel_id=1, source_target_pairs={{0,8},{4,12},{8,0},{12,4},{16,24},{20,28},{24,16},{28,20},{1,9},{5... | collective-permute-start | bytes 1671176 | tf_op jit(solution)/shard_map/ppermute | solution.py:33
  322.3 35.0 %collective-permute-start.31 = (bf16[256,2048]{1,0:T(8,128)(2,1)S(1)}, bf16[256,2048]{1,0:T(8,128)(2,1)S(1)}, u32[]{:S(2)}, u32[]{:S(2)}) collective-permute-start(bf16[256,2048]{1,0:T(8,128)(2,1)S(1)} %pad_maximum_fusion.5), channel_id=1, source_target_pairs={{0,16},{4,20},{8,24},{12,28},{16,0},{20,4},{24,8},{28,12},{1,17},{... | collective-permute-start | bytes 3145736 | tf_op jit(solution)/shard_map/ppermute | solution.py:33
  330.7 26.7 %collective-permute-start.28 = (bf16[256,2048]{1,0:T(8,128)(2,1)S(1)}, bf16[256,2048]{1,0:T(8,128)(2,1)S(1)}, u32[]{:S(2)}, u32[]{:S(2)}) collective-permute-start(bf16[256,2048]{1,0:T(8,128)(2,1)S(1)} %pad_maximum_fusion.4), channel_id=1, source_target_pairs={{0,8},{4,12},{8,0},{12,4},{16,24},{20,28},{24,16},{28,20},{1,9},{5... | collective-permute-start | bytes 3145736 | tf_op jit(solution)/shard_map/ppermute | solution.py:33
  334.9 44.4 %collective-permute-start.55 = (bf16[256,2176]{1,0:T(8,128)(2,1)S(1)}, bf16[256,2176]{1,0:T(8,128)(2,1)S(1)}, u32[]{:S(2)}, u32[]{:S(2)}) collective-permute-start(bf16[256,2176]{1,0:T(8,128)(2,1)S(1)} %pad_maximum_fusion.1), channel_id=1, source_target_pairs={{0,16},{4,20},{8,24},{12,28},{16,0},{20,4},{24,8},{28,12},{1,17},{... | collective-permute-start | bytes 3342344 | tf_op jit(solution)/shard_map/ppermute | solution.py:33
  336.7 42.6 %collective-permute-start.52 = (bf16[256,2176]{1,0:T(8,128)(2,1)S(1)}, bf16[256,2176]{1,0:T(8,128)(2,1)S(1)}, u32[]{:S(2)}, u32[]{:S(2)}) collective-permute-start(bf16[256,2176]{1,0:T(8,128)(2,1)S(1)} %pad_maximum_fusion), channel_id=1, source_target_pairs={{0,8},{4,12},{8,0},{12,4},{16,24},{20,28},{24,16},{28,20},{1,9},{5... | collective-permute-start | bytes 3342344 | tf_op jit(solution)/shard_map/ppermute | solution.py:33
  415.8 107.9 %collective-permute-start.35 = (bf16[64,2048]{1,0:T(8,128)(2,1)}, bf16[64,2048]{1,0:T(8,128)(2,1)}, u32[]{:S(2)}, u32[]{:S(2)}) collective-permute-start(bf16[64,2048]{1,0:T(8,128)(2,1)} %pad_maximum_fusion.18), channel_id=1, source_target_pairs={{0,3},{1,0},{2,1},{3,2},{4,7},{5,4},{6,5},{7,6},{8,11},{9,8},{10,9... | collective-permute-start | bytes 786440 | tf_op jit(solution)/shard_map/ppermute | solution.py:37
  424.7 39.0 %collective-permute-start.63 = (bf16[64,1024]{1,0:T(8,128)(2,1)S(1)}, bf16[64,1024]{1,0:T(8,128)(2,1)S(1)}, u32[]{:S(2)}, u32[]{:S(2)}) collective-permute-start(bf16[64,1024]{1,0:T(8,128)(2,1)S(1)} %slice.490), channel_id=1, source_target_pairs={{0,3},{1,0},{2,1},{3,2},{4,7},{5,4},{6,5},{7,6},{8,11},{9,8},{10,9... | collective-permute-start | bytes 393224 | tf_op jit(solution)/shard_map/ppermute | solution.py:37
  428.1 35.6 %collective-permute-start.62 = (bf16[64,1024]{1,0:T(8,128)(2,1)S(1)}, bf16[64,1024]{1,0:T(8,128)(2,1)S(1)}, u32[]{:S(2)}, u32[]{:S(2)}) collective-permute-start(bf16[64,1024]{1,0:T(8,128)(2,1)S(1)} %slice.489), channel_id=1, source_target_pairs={{0,1},{1,2},{2,3},{3,0},{4,5},{5,6},{6,7},{7,4},{8,9},{9,10},{10,1... | collective-permute-start | bytes 393224 | tf_op jit(solution)/shard_map/ppermute | solution.py:37
  510.9 86.7 %collective-permute-start.79 = (bf16[256,1280]{1,0:T(8,128)(2,1)}, bf16[256,1280]{1,0:T(8,128)(2,1)}, u32[]{:S(2)}, u32[]{:S(2)}) collective-permute-start(bf16[256,1280]{1,0:T(8,128)(2,1)} %get-tuple-element.104), channel_id=1, source_target_pairs={{0,4},{4,0},{8,12},{12,8},{16,20},{20,16},{24,28},{28,24},{1,5},{5... | collective-permute-start | bytes 1966088 | tf_op jit(solution)/shard_map/ppermute | solution.py:33
  511.9 80.7 %collective-permute-start.80 = (bf16[256,1280]{1,0:T(8,128)(2,1)}, bf16[256,1280]{1,0:T(8,128)(2,1)}, u32[]{:S(2)}, u32[]{:S(2)}) collective-permute-start(bf16[256,1280]{1,0:T(8,128)(2,1)} %get-tuple-element.104), channel_id=1, source_target_pairs={{0,8},{4,12},{8,0},{12,4},{16,24},{20,28},{24,16},{28,20},{1,9},{5... | collective-permute-start | bytes 1966088 | tf_op jit(solution)/shard_map/ppermute | solution.py:33
  521.3 70.1 %collective-permute-start.82 = (bf16[256,1280]{1,0:T(8,128)(2,1)}, bf16[256,1280]{1,0:T(8,128)(2,1)}, u32[]{:S(2)}, u32[]{:S(2)}) collective-permute-start(bf16[256,1280]{1,0:T(8,128)(2,1)} %get-tuple-element.104), channel_id=1, source_target_pairs={{0,16},{4,20},{8,24},{12,28},{16,0},{20,4},{24,8},{28,12},{1,17},{... | collective-permute-start | bytes 1966088 | tf_op jit(solution)/shard_map/ppermute | solution.py:33
  528.7 43.4 %collective-permute-start.36 = (bf16[64,2048]{1,0:T(8,128)(2,1)}, bf16[64,2048]{1,0:T(8,128)(2,1)S(1)}, u32[]{:S(2)}, u32[]{:S(2)}) collective-permute-start(bf16[64,2048]{1,0:T(8,128)(2,1)} %get-tuple-element.107), channel_id=1, source_target_pairs={{0,3},{1,0},{2,1},{3,2},{4,7},{5,4},{6,5},{7,6},{8,11},{9,8},{10,9... | collective-permute-start | bytes 786440 | tf_op jit(solution)/shard_map/ppermute | solution.py:37
  528.8 44.9 %collective-permute-start.37 = (bf16[64,2048]{1,0:T(8,128)(2,1)}, bf16[64,2048]{1,0:T(8,128)(2,1)S(1)}, u32[]{:S(2)}, u32[]{:S(2)}) collective-permute-start(bf16[64,2048]{1,0:T(8,128)(2,1)} %get-tuple-element.107), channel_id=1, source_target_pairs={{0,1},{1,2},{2,3},{3,0},{4,5},{5,6},{6,7},{7,4},{8,9},{9,10},{10,1... | collective-permute-start | bytes 786440 | tf_op jit(solution)/shard_map/ppermute | solution.py:37
  (189 other events, 2387.7 us)
Sparse Core Ops, SparseCore 0:
  416.9 32.4 reduce-scatter.1
